TPU v7x, 128 devices: a whole 4x4x4 slice. The times are simulated.
128 devices in a mesh: atom: 16 (over y, x), mode: 8 (over z, core).
Axes of the slice: x: 4, y: 4, z: 4, core: 2. Of those that a mesh axis runs over, the one named last changes fastest.
Arguments:
- eigvec: bfloat16 [3, 4096, 2048], P(None, 'atom', 'mode'), may hold values from -0.0546875 to 0.0546875
- force: float32 [3, 3, 16, 4096], P(None, None, None, 'atom'), may hold values from -12 to 12
- bond: float32 [3, 16, 4096], P(None, None, 'atom'), may hold values from -6 to 6
- nbr: int32 [16, 4096], P(None, 'atom'), may hold values from 0 to 4095, as said below
- band: int32 [2, 2048], P(None, 'mode'), may hold values from 0 to 2048, as said below
- freq: float32 [2048], P('mode'), may hold values from 0.5 to 4, as said below
Outputs:
- diffusivity: float32 [2048], P('mode')
- conductivity: float32 [2048], P('mode')
Inputs may be any that keep to these rules, and one draw needn't show every extreme that they name: `nbr`: each entry is an atom whose position in atom order differs from that of its own atom by 1 to 128, counted cyclically over the 4096 atoms; the distance 128 occurs in every draw. For every mode i: max(0, i - 128) <= band[0, i] <= i < band[1, i] <= min(2048, i + 129); both outer limits are reached at some mode. `freq`: strictly increasing along the modes.
All inputs are finite; a program needn't handle non-finite values.
Results may differ from a plain program's by a relative error of at most 0.00057.
Values may be sent and summed in bfloat16 or wider, within the bound.
A program may use at most 64 MiB of HBM per device.

v0:
```python
import math
import jax
import jax.numpy as jnp
from jax import lax
from jax.sharding import PartitionSpec as P

ATOM_DEV = 256
MODE_DEV = 256
RIM = 128
HALF = 128
BROAD = 128


def extended(shard, sides, width, wrap):
    for axis, dim in sides:
        size, length = (lax.axis_size(axis), shard.shape[dim])
        up = [(i, (i + 1) % size) for i in range(size if wrap else size - 1)]
        down = [(j, i) for i, j in up]
        last = lax.slice_in_dim(shard, length - width, length, axis=dim)
        first = lax.slice_in_dim(shard, 0, width, axis=dim)
        before = lax.ppermute(last, axis, up)
        after = lax.ppermute(first, axis, down)
        shard = jnp.concatenate([before, shard, after], axis=dim)
    return shard


def prefix(part, axis, combine, identity):
    place = lax.axis_index(axis)
    gathered = lax.all_gather(part, axis)
    state = jnp.zeros_like(part) + jnp.asarray(identity, part.dtype)

    def one(lap, state):
        return combine(state, lax.dynamic_index_in_dim(gathered, lap, 0, False))

    return lax.fori_loop(0, place, one, state)


def capacity_of(spectral):
    return spectral * spectral * jnp.exp(spectral) / jnp.expm1(spectral) ** 2


def pair_weight(own_freq, partner_freq, own_ids, partner_ids, lower_end, upper_end, broaden):
    inside = (
        (partner_ids[:, None] >= lower_end[None, :])
        & (partner_ids[:, None] < upper_end[None, :])
        & (partner_ids[:, None] != own_ids[None, :])
    )
    detune = own_freq[None, :] - partner_freq[:, None]
    lorentz = broaden / math.pi / (detune * detune + broaden * broaden)
    factor = (own_freq[None, :] + partner_freq[:, None]) ** 2 / (
        4.0 * own_freq[None, :] * partner_freq[:, None]
    )
    return jnp.where(inside, lorentz * factor, 0.0)


def add_totals(earlier, later):
    return earlier + later


def body(eigvec, force, bond, nbr, band, freq):
    atom_count = ATOM_DEV * lax.axis_size("atom")
    mode_count = MODE_DEV * lax.axis_size("mode")
    partner_span = MODE_DEV + 2 * HALF
    spectrum = lax.all_gather(freq, "mode", axis=0, tiled=True)
    atom_rows = extended(eigvec, (("atom", 1),), RIM, True)
    band_rows = extended(eigvec, (("mode", 2),), HALF, False)
    row_major = jnp.transpose(atom_rows, (1, 0, 2))
    domain = lax.axis_index("atom")
    local_ids = (nbr - domain * ATOM_DEV + RIM + atom_count) % atom_count
    block_size = min(512, ATOM_DEV)
    gathered = jnp.take(row_major, local_ids, axis=0)
    coupling = (bond[:, None, None, :, 0:block_size] * force[None, :, :, :, 0:block_size]).astype(
        jnp.bfloat16
    )
    block_image = jnp.einsum(
        "kcdna,nadi->kcai", coupling, gathered, preferred_element_type=jnp.float32
    )
    pieces = block_image.astype(jnp.bfloat16)
    pair_terms = jnp.einsum("caj,kcai->kji", band_rows, pieces, preferred_element_type=jnp.float32)
    mode_block = lax.axis_index("mode")
    mode_start = mode_block * MODE_DEV
    broaden = BROAD * (jnp.max(spectrum) - jnp.min(spectrum)) / (mode_count - 1)
    padded_freq = jnp.pad(spectrum, (HALF, HALF), constant_values=1.0)
    partner_freq = lax.dynamic_slice_in_dim(padded_freq, mode_start, partner_span)
    partner_ids = mode_start - HALF + jnp.arange(partner_span, dtype=jnp.int32)
    own_ids = mode_start + jnp.arange(MODE_DEV, dtype=jnp.int32)
    weight = pair_weight(freq, partner_freq, own_ids, partner_ids, band[0], band[1], broaden)
    summed_pair = lax.psum(pair_terms, "atom")
    strength = jnp.sum(summed_pair * summed_pair, axis=0)
    row_sums = jnp.sum(weight * strength, axis=0)
    diffusivity = math.pi / (3.0 * freq * freq) * row_sums
    running = jnp.cumsum(capacity_of(freq) * diffusivity)
    device_total = running[-1]
    earlier_sum = prefix(device_total, "mode", add_totals, jnp.float32(0.0))
    conductivity = (earlier_sum + running) / MODE_DEV
    return (diffusivity, conductivity)


def solution(mesh):
    in_specs = (
        P(None, "atom", "mode"),
        P(None, None, None, "atom"),
        P(None, None, "atom"),
        P(None, "atom"),
        P(None, "mode"),
        P("mode"),
    )
    out_specs = (P("mode"), P("mode"))
    return jax.shard_map(body, mesh=mesh, in_specs=in_specs, out_specs=out_specs, check_vma=False)
```

profile of v0, /device:TPU:97, one launch (start us, length us, event | category | flops | bytes accessed | tf_op | source)
XLA Modules:
  0.0 190.9 jit_solution(17926169755393144528)
XLA Ops:
  7.2 0.0 copy-start
  7.2 0.0 copy-start.3
  7.2 0.0 copy-start.2
  7.2 0.0 all-reduce.4.cloned.1.call-start
  7.2 1.4 copy.12
  8.6 0.0 copy-start.4
  8.6 0.2 fusion.21
  8.8 5.0 %collective-permute-start.1 = (bf16[3,128,256]{2,0,1:T(4,128)(2,1)S(1)}, bf16[3,128,256]{2,0,1:T(4,128)(2,1)}, u32[]{:S(2)}, u32[]{:S(2)}) collective-permute-start(bf16[3,128,256]{2,0,1:T(4,128)(2,1)S(1)} %get-tuple-element.39), channel_id=1, source_target_pairs={{8,0},{16,8},{24,16},{32,24},{40,32},{48,40},{56,48},{64,56},{72,6... | collective-permute-start | bytes 589832 | tf_op jit(solution)/shard_map/ppermute | solution.py:22
  13.8 0.0 collective-permute-start
  13.8 0.8 fusion.22
  14.7 3.5 %collective-permute-start.3 = (bf16[3,256,128]{2,1,0:T(8,128)(2,1)}, bf16[3,256,128]{2,1,0:T(8,128)(2,1)}, u32[]{:S(2)}, u32[]{:S(2)}) collective-permute-start(bf16[3,256,128]{2,1,0:T(8,128)(2,1)} %get-tuple-element.41), channel_id=1, source_target_pairs={{1,0},{2,1},{3,2},{4,3},{5,4},{6,5},{7,6},{9,8},{10,9},{11,10},{12... | collective-permute-start | bytes 589832 | tf_op jit(solution)/shard_map/ppermute | solution.py:22
  18.2 1.3 collective-permute-start.2
  19.6 0.7 copy.17
  20.3 1.1 copy.16
  21.4 0.7 copy.11
  22.1 0.0 collective-permute-done.1
  22.1 2.1 %collective-permute-done = bf16[3,128,256]{2,0,1:T(4,128)(2,1)} collective-permute-done((bf16[3,128,256]{2,0,1:T(4,128)(2,1)S(1)}, bf16[3,128,256]{2,0,1:T(4,128)(2,1)}, u32[]{:S(2)}, u32[]{:S(2)}) %collective-permute-start) | collective-permute-done | bytes 196640 | tf_op jit(solution)/shard_map/ppermute | solution.py:21
  24.2 1.8 maximum_bitcast_fusion
  25.9 32.8 %gather_fusion = bf16[4096,3,256]{2,1,0:T(4,128)(2,1)} fusion(bf16[512,3,256]{2,1,0:T(4,128)(2,1)S(1)} %maximum_bitcast_fusion, s32[4096]{0:T(1024)S(1)} %broadcast_clamp_fusion), kind=kCustom, calls=%fused_computation | custom fusion | bytes 12599296 | tf_op jit(solution)/shard_map/jit(_take)/gather | solution.py:71
  58.7 9.2 %fusion.8 = bf16[3,3,256,256]{3,1,0,2:T(4,128)(2,1)S(1)} fusion(f32[3,3,16,256]{2,0,1,3:T(4,128)S(1)} %copy.17, f32[3,16,256]{1,0,2:T(4,128)S(1)} %copy-done.1, bf16[16,256,3,256]{3,2,1,0:T(4,128)(2,1)} %bitcast.42, pred[16,256]{0,1:T(8,128)(4,1)} %copy.11), kind=kOutput, calls=%fused_computation.11 | convolution fusion | flops 60579840 | bytes 7671808 | tf_op jit(solution)/shard_map/kcdna,nadi->kcai/dot_general | solution.py:75
  67.9 0.0 collective-permute-done.3
  67.9 0.0 collective-permute-done.2
  68.0 3.0 %convolution_bitcast_fusion = f32[3,512,256]{1,2,0:T(8,128)} fusion(bf16[3,3,256,256]{3,1,0,2:T(4,128)(2,1)S(1)} %fusion.8, bf16[3,256,128]{2,1,0:T(8,128)(2,1)} %collective-permute-done.3, bf16[3,256,256]{2,1,0:T(8,128)(2,1)S(1)} %copy-done, bf16[3,256,128]{2,1,0:T(8,128)(2,1)} %collective-permute-done.2), kind=kOutput, calls=%fused_computation.12 | convolution fusion | flops 606339072 | bytes 3538944 | tf_op jit(solution)/shard_map/caj,kcai->kji/dot_general | solution.py:79
  71.0 0.0 all-reduce.4.cloned.1.call-update
  71.0 0.6 copy-done.5
  71.6 8.7 %all-gather = f32[8,1,256]{2,1,0:T(1,128)S(1)} all-gather(f32[1,1,256]{2,1,0:T(1,128)S(1)} %bitcast.45), channel_id=1, replica_groups=mesh['atom'=16,'mode'=8] {'mode'}, dimensions={0}, use_global_device_ids=true | all-gather | bytes 9216 | tf_op jit(solution)/shard_map/all_gather | solution.py:64
  80.3 0.6 fusion.20
  82.3 0.6 dynamic-slice
  82.9 0.1 pad_dynamic-slice_fusion
  83.0 74.9 %all-reduce.4.cloned.1.call-done = f32[3,512,256]{1,2,0:T(8,128)} async-done(((f32[3,512,256]{1,2,0:T(8,128)}), f32[3,512,256]{1,2,0:T(8,128)}) %all-reduce.4.cloned.1.call-update) | async-done | bytes 1572880 | tf_op jit(solution)/shard_map/psum | solution.py:88
  157.8 1.6 multiply_reduce_fusion
  159.5 0.5 multiply_reduce_fusion.1
  160.0 0.6 multiply_bitcast_fusion
  160.6 0.3 reduce-window.9
  160.9 0.1 slice.34
  161.0 0.1 slice_reduce_fusion
  161.1 0.1 add_bitcast_fusion
  161.2 0.8 slice_dynamic-update-slice_fusion
  162.0 11.9 %all-reduce.1 = f32[8]{0:T(128)S(1)} all-reduce(f32[8]{0:T(128)S(1)} %slice_dynamic-update-slice_fusion), channel_id=1, replica_groups=mesh['atom'=16,'mode'=8] {'mode'}, use_global_device_ids=true, to_apply=%add.1 | all-reduce | flops 8 | bytes 64
  173.8 9.7 %while.10 = (s32[]{:T(128)}, f32[]{:T(128)}, s32[]{:T(128)}, f32[8]{0:T(128)S(1)}, s32[]{:T(128)}, /*index=5*/s32[]{:T(128)}, s32[]{:T(128)}) while((s32[]{:T(128)}, f32[]{:T(128)}, s32[]{:T(128)}, f32[8]{0:T(128)S(1)}, s32[]{:T(128)}, /*index=5*/s32[]{:T(128)}, s32[]{:T(128)}) %tuple.27), condition=%wide.region_8.9_spmd, body=%wide.region_7.8_spmd.sunk | while | flops 6 | bytes 143 | solution.py:35
  173.8 0.7 dynamic_slice.10
  175.2 0.7 dynamic_slice.10
  176.6 0.7 dynamic_slice.10
  178.0 0.7 dynamic_slice.10
  179.4 0.7 dynamic_slice.10
  180.8 0.7 dynamic_slice.10
  182.1 0.7 dynamic_slice.10
  183.5 0.6 add_multiply_fusion
  (21 shorter events, 0.1 us)
Async XLA Ops:
  7.2 6.7 %copy-start = (bf16[3,256,256]{2,1,0:T(8,128)(2,1)S(1)}, bf16[3,256,256]{2,1,0:T(8,128)(2,1)}, u32[]{:S(2)}) copy-start(bf16[3,256,256]{2,1,0:T(8,128)(2,1)} %param.8) | copy-start | bytes 1179652
  7.2 12.3 %copy-start.3 = (s32[16,256]{1,0:T(8,128)S(1)}, s32[16,256]{1,0:T(8,128)}, u32[]{:S(2)}) copy-start(s32[16,256]{1,0:T(8,128)} %param.11) | copy-start | bytes 49156
  7.2 12.4 %copy-start.2 = (f32[3,3,16,256]{3,2,1,0:T(8,128)S(1)}, f32[3,3,16,256]{3,2,1,0:T(8,128)}, u32[]{:S(2)}) copy-start(f32[3,3,16,256]{3,2,1,0:T(8,128)} %param.9) | copy-start | bytes 442372
  7.2 150.6 %all-reduce.4.cloned.1.call-start = ((), (), s32[]{:S(2)}) async-start(), calls=%async_computation | async-start | bytes 3145728 | tf_op jit(solution)/shard_map/psum | solution.py:88
  8.6 11.7 %copy-start.4 = (f32[3,16,256]{2,1,0:T(8,128)S(1)}, f32[3,16,256]{2,1,0:T(8,128)}, u32[]{:S(2)}) copy-start(f32[3,16,256]{2,1,0:T(8,128)} %param.10) | copy-start | bytes 147460
  8.8 13.3 %collective-permute-start.1 = (bf16[3,128,256]{2,0,1:T(4,128)(2,1)S(1)}, bf16[3,128,256]{2,0,1:T(4,128)(2,1)}, u32[]{:S(2)}, u32[]{:S(2)}) collective-permute-start(bf16[3,128,256]{2,0,1:T(4,128)(2,1)S(1)} %get-tuple-element.39), channel_id=1, source_target_pairs={{8,0},{16,8},{24,16},{32,24},{40,32},{48,40},{56,48},{64,56},{72,6... | collective-permute-start | bytes 589832 | tf_op jit(solution)/shard_map/ppermute | solution.py:22
  13.8 10.3 %collective-permute-start = (bf16[3,128,256]{2,0,1:T(4,128)(2,1)S(1)}, bf16[3,128,256]{2,0,1:T(4,128)(2,1)}, u32[]{:S(2)}, u32[]{:S(2)}) collective-permute-start(bf16[3,128,256]{2,0,1:T(4,128)(2,1)S(1)} %get-tuple-element.38), channel_id=1, source_target_pairs={{0,8},{8,16},{16,24},{24,32},{32,40},{40,48},{48,56},{56,64},{64,7... | collective-permute-start | bytes 589832 | tf_op jit(solution)/shard_map/ppermute | solution.py:21
  14.7 53.3 %collective-permute-start.3 = (bf16[3,256,128]{2,1,0:T(8,128)(2,1)}, bf16[3,256,128]{2,1,0:T(8,128)(2,1)}, u32[]{:S(2)}, u32[]{:S(2)}) collective-permute-start(bf16[3,256,128]{2,1,0:T(8,128)(2,1)} %get-tuple-element.41), channel_id=1, source_target_pairs={{1,0},{2,1},{3,2},{4,3},{5,4},{6,5},{7,6},{9,8},{10,9},{11,10},{12... | collective-permute-start | bytes 589832 | tf_op jit(solution)/shard_map/ppermute | solution.py:22
  18.2 49.7 %collective-permute-start.2 = (bf16[3,256,128]{2,1,0:T(8,128)(2,1)}, bf16[3,256,128]{2,1,0:T(8,128)(2,1)}, u32[]{:S(2)}, u32[]{:S(2)}) collective-permute-start(bf16[3,256,128]{2,1,0:T(8,128)(2,1)} %get-tuple-element.40), channel_id=1, source_target_pairs={{0,1},{1,2},{2,3},{3,4},{4,5},{5,6},{6,7},{8,9},{9,10},{10,11},{11... | collective-permute-start | bytes 589832 | tf_op jit(solution)/shard_map/ppermute | solution.py:21
  25.9 32.8 %copy-start.1 = (f32[3,16,256]{1,0,2:T(4,128)S(1)}, f32[3,16,256]{1,0,2:T(4,128)}, u32[]{:S(2)}) copy-start(f32[3,16,256]{1,0,2:T(4,128)} %copy.16) | copy-start | bytes 147460
  71.0 0.7 copy-start.5
  71.0 11.3 %copy-start.7 = (u32[128]{0:T(128)S(1)}, u32[128]{0:T(128)}, u32[]{:S(2)}) copy-start(u32[128]{0:T(128)} %constant.93) | copy-start | bytes 1540
  71.0 12.0 %copy-start.6 = (s32[2,256]{1,0:T(2,128)S(1)}, s32[2,256]{1,0:T(2,128)}, u32[]{:S(2)}) copy-start(s32[2,256]{1,0:T(2,128)} %param.12) | copy-start | bytes 6148
Sparse Core Ops, SparseCore 0:
  71.1 86.6 all-reduce.3
where the time goes:
time: 191 us
  waiting for transfers between devices  76.9 us (40%)
  local copies, waits for them, and re-layouts  44.7 us (23%)
  blocking collectives  20.6 us (11%)
  between operations  15.5 us (8%)
  matrix products  12.2 us (6%)
  starting transfers between devices  9.86 us (5%)
  other arithmetic  6.15 us (3%)
  loops' own time  5 us (3%)
    psum x1, waiting for transfers between devices, body(): summed_pair = lax.psum(pair_terms, 'atom')  74.9 us
    gather x1, local copies, waits for them, and re-layouts, body(): gathered = jnp.take(row_major, local_ids, axis=0)  32.8 us
    unnamed x1, blocking collectives  11.9 us
    dot_general x1, matrix products, body(): jnp.einsum('kcdna,nadi->kcai', coupling, gathered, preferred_element_type...  9.23 us
    all_gather x1, blocking collectives, body(): spectrum = lax.all_gather(freq, 'mode', axis=0, tiled=True)  8.7 us
    ppermute x2, starting transfers between devices, extended(): after = lax.ppermute(first, axis, down)  8.54 us
    unnamed x23, local copies, waits for them, and re-layouts  5.23 us
    another operation x1, loops' own time, prefix(): return lax.fori_loop(0, place, one, state)  5 us
  transfers between devices with their start and end apart: 5, of which 2 were waited for; matrix products, arithmetic and copies ran while one was open for 25% of the time, Pallas kernels for 0%

commit v1 on v0

--- a/solution.py
+++ b/solution.py
@@ -85,7 +85,10 @@
     partner_ids = mode_start - HALF + jnp.arange(partner_span, dtype=jnp.int32)
     own_ids = mode_start + jnp.arange(MODE_DEV, dtype=jnp.int32)
     weight = pair_weight(freq, partner_freq, own_ids, partner_ids, band[0], band[1], broaden)
-    summed_pair = lax.psum(pair_terms, "atom")
+    n_dev, summed_pair = (lax.axis_size("atom"), pair_terms)
+    for stride in [1 << k for k in range(n_dev.bit_length() - 1)]:
+        swap = [(i_2, i_2 ^ stride) for i_2 in range(n_dev)]
+        summed_pair = summed_pair + lax.ppermute(summed_pair, "atom", swap)
     strength = jnp.sum(summed_pair * summed_pair, axis=0)
     row_sums = jnp.sum(weight * strength, axis=0)
     diffusivity = math.pi / (3.0 * freq * freq) * row_sums

time: 191 us -> 230 us (1.20)
  waiting for transfers between devices: 76.9 us -> 120 us
  between operations: 15.5 us -> 2.15 us
  blocking collectives: 20.6 us -> 29.4 us
  starting transfers between devices: 9.86 us -> 12.8 us
    ppermute x0 -> x4, waiting for transfers between devices: none -> 120 us  [body(): summed_pair = summed_pair + lax.ppermute(summed_pair, 'atom', swap)]
    psum x1 -> x0, waiting for transfers between devices: 74.9 us -> none  [body(): summed_pair = lax.psum(pair_terms, 'atom')]
    unnamed x1, blocking collectives: 11.9 us -> 17 us
    all_gather x1, blocking collectives: 8.7 us -> 12.5 us  [body(): spectrum = lax.all_gather(freq, 'mode', axis=0, tiled=True)]
  transfers between devices with their start and end apart: 5 -> 8, of which waited for: 2 -> 4; matrix products, arithmetic and copies ran while one was open for 25% -> 21% of each run, Pallas kernels for 0% -> 0%
where the time goes in v1:
time: 230 us; the launch traced here: 229 us
  waiting for transfers between devices  120 us (52%)
  local copies, waits for them, and re-layouts  43.5 us (19%)
  blocking collectives  29.4 us (13%)
  starting transfers between devices  12.8 us (6%)
  matrix products  11.1 us (5%)
  other arithmetic  5.95 us (3%)
  loops' own time  4.12 us (2%)
    ppermute x4, waiting for transfers between devices, body(): summed_pair = summed_pair + lax.ppermute(summed_pair, 'atom', swap)  120 us
    gather x1, local copies, waits for them, and re-layouts, body(): gathered = jnp.take(row_major, local_ids, axis=0)  32.8 us
    unnamed x1, blocking collectives  17 us
    all_gather x1, blocking collectives, body(): spectrum = lax.all_gather(freq, 'mode', axis=0, tiled=True)  12.5 us
    dot_general x1, matrix products, body(): jnp.einsum('kcdna,nadi->kcai', coupling, gathered, preferred_element_type...  9.23 us
    ppermute x2, starting transfers between devices, extended(): after = lax.ppermute(first, axis, down)  8.04 us
    unnamed x23, local copies, waits for them, and re-layouts  4.62 us
  transfers between devices with their start and end apart: 8, of which 4 were waited for; matrix products, arithmetic and copies ran while one was open for 21% of the time, Pallas kernels for 0%

profile of v1, /device:TPU:97, one launch (start us, length us, event | category | flops | bytes accessed | tf_op | source)
XLA Modules:
  0.0 229.4 jit_solution(5761367130808095341)
XLA Ops:
  0.7 1.4 copy.12
  2.1 0.2 fusion.21
  2.3 1.3 collective-permute-start
  3.5 3.8 %collective-permute-start.1 = (bf16[3,128,256]{2,0,1:T(4,128)(2,1)S(1)}, bf16[3,128,256]{2,0,1:T(4,128)(2,1)}, u32[]{:S(2)}, u32[]{:S(2)}) collective-permute-start(bf16[3,128,256]{2,0,1:T(4,128)(2,1)S(1)} %get-tuple-element.39), channel_id=1, source_target_pairs={{8,0},{16,8},{24,16},{32,24},{40,32},{48,40},{56,48},{64,56},{72,6... | collective-permute-start | bytes 589832 | tf_op jit(solution)/shard_map/ppermute | solution.py:22
  7.3 0.9 fusion.22
  8.2 1.3 collective-permute-start.2
  9.5 4.2 %collective-permute-start.3 = (bf16[3,256,128]{2,1,0:T(8,128)(2,1)}, bf16[3,256,128]{2,1,0:T(8,128)(2,1)}, u32[]{:S(2)}, u32[]{:S(2)}) collective-permute-start(bf16[3,256,128]{2,1,0:T(8,128)(2,1)} %get-tuple-element.41), channel_id=1, source_target_pairs={{1,0},{2,1},{3,2},{4,3},{5,4},{6,5},{7,6},{9,8},{10,9},{11,10},{12... | collective-permute-start | bytes 589832 | tf_op jit(solution)/shard_map/ppermute | solution.py:22
  13.8 0.7 copy.11
  14.5 0.7 copy.17
  15.3 1.1 copy.16
  16.3 1.8 maximum_bitcast_fusion
  18.1 32.8 %gather_fusion = bf16[4096,3,256]{2,1,0:T(4,128)(2,1)} fusion(bf16[512,3,256]{2,1,0:T(4,128)(2,1)S(1)} %maximum_bitcast_fusion, s32[4096]{0:T(1024)S(1)} %broadcast_clamp_fusion), kind=kCustom, calls=%fused_computation | custom fusion | bytes 12599296 | tf_op jit(solution)/shard_map/jit(_take)/gather | solution.py:71
  50.9 9.2 %fusion.8 = bf16[3,3,256,256]{3,1,0,2:T(4,128)(2,1)S(1)} fusion(f32[3,3,16,256]{2,0,1,3:T(4,128)S(1)} %copy.17, f32[3,16,256]{1,0,2:T(4,128)S(1)} %copy-done.1, bf16[16,256,3,256]{3,2,1,0:T(4,128)(2,1)} %bitcast.42, pred[16,256]{0,1:T(8,128)(4,1)} %copy.11), kind=kOutput, calls=%fused_computation.11 | convolution fusion | flops 60579840 | bytes 7671808 | tf_op jit(solution)/shard_map/kcdna,nadi->kcai/dot_general | solution.py:75
  60.1 1.8 convolution_bitcast_fusion
  62.0 0.1 collective-permute-start.4
  62.1 34.9 %collective-permute-done.4 = f32[3,512,256]{1,2,0:T(8,128)S(1)} collective-permute-done((f32[3,512,256]{1,2,0:T(8,128)S(1)}, f32[3,512,256]{1,2,0:T(8,128)S(1)}, u32[]{:S(2)}, u32[]{:S(2)}) %collective-permute-start.4) | collective-permute-done | bytes 1572896 | tf_op jit(solution)/shard_map/ppermute | solution.py:91
  96.9 0.3 add.106
  97.3 0.1 collective-permute-start.5
  97.4 35.5 %collective-permute-done.5 = f32[3,512,256]{1,2,0:T(8,128)S(1)} collective-permute-done((f32[3,512,256]{1,2,0:T(8,128)S(1)}, f32[3,512,256]{1,2,0:T(8,128)S(1)}, u32[]{:S(2)}, u32[]{:S(2)}) %collective-permute-start.5) | collective-permute-done | bytes 1572896 | tf_op jit(solution)/shard_map/ppermute | solution.py:91
  132.9 0.3 add.107
  133.2 0.0 copy-start.7
  133.3 0.2 collective-permute-start.6
  133.4 33.1 %collective-permute-done.6 = f32[3,512,256]{1,2,0:T(8,128)S(1)} collective-permute-done((f32[3,512,256]{1,2,0:T(8,128)S(1)}, f32[3,512,256]{1,2,0:T(8,128)S(1)}, u32[]{:S(2)}, u32[]{:S(2)}) %collective-permute-start.6) | collective-permute-done | bytes 1572896 | tf_op jit(solution)/shard_map/ppermute | solution.py:91
  166.5 0.3 add.108
  166.8 1.8 collective-permute-start.7
  168.7 12.5 %all-gather = f32[8,1,256]{2,1,0:T(1,128)S(1)} all-gather(f32[1,1,256]{2,1,0:T(1,128)S(1)} %bitcast.45), channel_id=1, replica_groups=mesh['atom'=16,'mode'=8] {'mode'}, dimensions={0}, use_global_device_ids=true | all-gather | bytes 9216 | tf_op jit(solution)/shard_map/all_gather | solution.py:64
  181.1 0.6 fusion.20
  183.0 0.6 dynamic-slice
  183.6 0.1 pad_dynamic-slice_fusion
  183.7 17.0 %collective-permute-done.7 = f32[3,512,256]{1,2,0:T(8,128)S(1)} collective-permute-done((f32[3,512,256]{1,2,0:T(8,128)S(1)}, f32[3,512,256]{1,2,0:T(8,128)S(1)}, u32[]{:S(2)}, u32[]{:S(2)}) %collective-permute-start.7) | collective-permute-done | bytes 1572896 | tf_op jit(solution)/shard_map/ppermute | solution.py:91
  200.7 0.4 multiply_reduce_fusion
  201.2 0.5 multiply_reduce_fusion.1
  201.7 0.6 multiply_bitcast_fusion
  202.3 0.3 reduce-window.9
  202.6 0.1 slice.34
  202.7 0.1 slice_reduce_fusion
  202.8 0.1 add_bitcast_fusion
  202.9 0.8 slice_dynamic-update-slice_fusion
  203.7 17.0 %all-reduce.1 = f32[8]{0:T(128)S(1)} all-reduce(f32[8]{0:T(128)S(1)} %slice_dynamic-update-slice_fusion), channel_id=1, replica_groups=mesh['atom'=16,'mode'=8] {'mode'}, use_global_device_ids=true, to_apply=%add.1 | all-reduce | flops 8 | bytes 64
  220.7 8.2 %while.10 = (s32[]{:T(128)}, f32[]{:T(128)}, s32[]{:T(128)}, f32[8]{0:T(128)S(1)}, s32[]{:T(128)}, /*index=5*/s32[]{:T(128)}, s32[]{:T(128)}) while((s32[]{:T(128)}, f32[]{:T(128)}, s32[]{:T(128)}, f32[8]{0:T(128)S(1)}, s32[]{:T(128)}, /*index=5*/s32[]{:T(128)}, s32[]{:T(128)}) %tuple.27), condition=%wide.region_7.8_spmd, body=%wide.region_6.7_spmd.sunk | while | flops 6 | bytes 135 | solution.py:35
  220.7 0.6 dynamic_slice.10
  221.8 0.6 dynamic_slice.10
  223.0 0.6 dynamic_slice.10
  224.2 0.6 dynamic_slice.10
  225.3 0.6 dynamic_slice.10
  226.5 0.6 dynamic_slice.10
  227.7 0.6 dynamic_slice.10
  228.8 0.6 add_multiply_fusion
  (29 shorter events, 0.2 us)
Async XLA Ops:
  0.6 6.7 %copy-start = (bf16[3,256,256]{2,1,0:T(8,128)(2,1)S(1)}, bf16[3,256,256]{2,1,0:T(8,128)(2,1)}, u32[]{:S(2)}) copy-start(bf16[3,256,256]{2,1,0:T(8,128)(2,1)} %param.8) | copy-start | bytes 1179652
  0.6 13.1 %copy-start.3 = (s32[16,256]{1,0:T(8,128)S(1)}, s32[16,256]{1,0:T(8,128)}, u32[]{:S(2)}) copy-start(s32[16,256]{1,0:T(8,128)} %param.11) | copy-start | bytes 49156
  0.6 13.9 %copy-start.2 = (f32[3,3,16,256]{3,2,1,0:T(8,128)S(1)}, f32[3,3,16,256]{3,2,1,0:T(8,128)}, u32[]{:S(2)}) copy-start(f32[3,3,16,256]{3,2,1,0:T(8,128)} %param.9) | copy-start | bytes 442372
  2.2 13.0 %copy-start.4 = (f32[3,16,256]{2,1,0:T(8,128)S(1)}, f32[3,16,256]{2,1,0:T(8,128)}, u32[]{:S(2)}) copy-start(f32[3,16,256]{2,1,0:T(8,128)} %param.10) | copy-start | bytes 147460
  2.3 14.1 %collective-permute-start = (bf16[3,128,256]{2,0,1:T(4,128)(2,1)S(1)}, bf16[3,128,256]{2,0,1:T(4,128)(2,1)}, u32[]{:S(2)}, u32[]{:S(2)}) collective-permute-start(bf16[3,128,256]{2,0,1:T(4,128)(2,1)S(1)} %get-tuple-element.38), channel_id=1, source_target_pairs={{0,8},{8,16},{16,24},{24,32},{32,40},{40,48},{48,56},{56,64},{64,7... | collective-permute-start | bytes 589832 | tf_op jit(solution)/shard_map/ppermute | solution.py:21
  3.5 12.8 %collective-permute-start.1 = (bf16[3,128,256]{2,0,1:T(4,128)(2,1)S(1)}, bf16[3,128,256]{2,0,1:T(4,128)(2,1)}, u32[]{:S(2)}, u32[]{:S(2)}) collective-permute-start(bf16[3,128,256]{2,0,1:T(4,128)(2,1)S(1)} %get-tuple-element.39), channel_id=1, source_target_pairs={{8,0},{16,8},{24,16},{32,24},{40,32},{48,40},{56,48},{64,56},{72,6... | collective-permute-start | bytes 589832 | tf_op jit(solution)/shard_map/ppermute | solution.py:22
  8.2 51.9 %collective-permute-start.2 = (bf16[3,256,128]{2,1,0:T(8,128)(2,1)}, bf16[3,256,128]{2,1,0:T(8,128)(2,1)}, u32[]{:S(2)}, u32[]{:S(2)}) collective-permute-start(bf16[3,256,128]{2,1,0:T(8,128)(2,1)} %get-tuple-element.40), channel_id=1, source_target_pairs={{0,1},{1,2},{2,3},{3,4},{4,5},{5,6},{6,7},{8,9},{9,10},{10,11},{11... | collective-permute-start | bytes 589832 | tf_op jit(solution)/shard_map/ppermute | solution.py:21
  9.5 50.6 %collective-permute-start.3 = (bf16[3,256,128]{2,1,0:T(8,128)(2,1)}, bf16[3,256,128]{2,1,0:T(8,128)(2,1)}, u32[]{:S(2)}, u32[]{:S(2)}) collective-permute-start(bf16[3,256,128]{2,1,0:T(8,128)(2,1)} %get-tuple-element.41), channel_id=1, source_target_pairs={{1,0},{2,1},{3,2},{4,3},{5,4},{6,5},{7,6},{9,8},{10,9},{11,10},{12... | collective-permute-start | bytes 589832 | tf_op jit(solution)/shard_map/ppermute | solution.py:22
  18.1 32.8 %copy-start.1 = (f32[3,16,256]{1,0,2:T(4,128)S(1)}, f32[3,16,256]{1,0,2:T(4,128)}, u32[]{:S(2)}) copy-start(f32[3,16,256]{1,0,2:T(4,128)} %copy.16) | copy-start | bytes 147460
  62.0 35.0 %collective-permute-start.4 = (f32[3,512,256]{1,2,0:T(8,128)S(1)}, f32[3,512,256]{1,2,0:T(8,128)S(1)}, u32[]{:S(2)}, u32[]{:S(2)}) collective-permute-start(f32[3,512,256]{1,2,0:T(8,128)S(1)} %convolution_bitcast_fusion), channel_id=1, source_target_pairs={{0,8},{8,0},{16,24},{24,16},{32,40},{40,32},{48,56},{56,48},{64,72... | collective-permute-start | bytes 4718600 | tf_op jit(solution)/shard_map/ppermute | solution.py:91
  97.3 35.6 %collective-permute-start.5 = (f32[3,512,256]{1,2,0:T(8,128)S(1)}, f32[3,512,256]{1,2,0:T(8,128)S(1)}, u32[]{:S(2)}, u32[]{:S(2)}) collective-permute-start(f32[3,512,256]{1,2,0:T(8,128)S(1)} %add.106), channel_id=1, source_target_pairs={{0,16},{8,24},{16,0},{24,8},{32,48},{40,56},{48,32},{56,40},{64,80... | collective-permute-start | bytes 4718600 | tf_op jit(solution)/shard_map/ppermute | solution.py:91
  133.2 35.4 %copy-start.5 = (f32[256]{0:T(256)S(1)}, f32[256]{0:T(256)}, u32[]{:S(2)}) copy-start(f32[256]{0:T(256)} %param.13) | copy-start | bytes 3076
  133.2 49.8 %copy-start.7 = (u32[128]{0:T(128)S(1)}, u32[128]{0:T(128)}, u32[]{:S(2)}) copy-start(u32[128]{0:T(128)} %constant.93) | copy-start | bytes 1540
  133.2 50.5 %copy-start.6 = (s32[2,256]{1,0:T(2,128)S(1)}, s32[2,256]{1,0:T(2,128)}, u32[]{:S(2)}) copy-start(s32[2,256]{1,0:T(2,128)} %param.12) | copy-start | bytes 6148
  133.3 33.2 %collective-permute-start.6 = (f32[3,512,256]{1,2,0:T(8,128)S(1)}, f32[3,512,256]{1,2,0:T(8,128)S(1)}, u32[]{:S(2)}, u32[]{:S(2)}) collective-permute-start(f32[3,512,256]{1,2,0:T(8,128)S(1)} %add.107), channel_id=1, source_target_pairs={{0,32},{8,40},{16,48},{24,56},{32,0},{40,8},{48,16},{56,24},{64,96... | collective-permute-start | bytes 4718600 | tf_op jit(solution)/shard_map/ppermute | solution.py:91
  166.8 33.9 %collective-permute-start.7 = (f32[3,512,256]{1,2,0:T(8,128)S(1)}, f32[3,512,256]{1,2,0:T(8,128)S(1)}, u32[]{:S(2)}, u32[]{:S(2)}) collective-permute-start(f32[3,512,256]{1,2,0:T(8,128)S(1)} %add.108), channel_id=1, source_target_pairs={{0,64},{8,72},{16,80},{24,88},{32,96},{40,104},{48,112},{56,120},{... | collective-permute-start | bytes 4718600 | tf_op jit(solution)/shard_map/ppermute | solution.py:91
